TPU v7x, 32 devices: a whole 2x2x4 slice. The times are simulated.
32 devices in a mesh: ch: 4 (over z), ha: 2 (over x), dp: 4 (over y, core).
Axes of the slice: x: 2, y: 2, z: 4, core: 2. Of those that a mesh axis runs over, the one named last changes fastest.
Arguments:
- features: bfloat16 [384, 4, 4, 4, 128], P('ch', 'dp', None, 'ha'), may hold values from -26 to 26
- frame_count: int32 [4], P('dp'), may hold values from 1 to 4, as said below
- norm1_gain: float32 [384], P('ch'), may hold values from 0.5 to 2
- norm1_shift: float32 [384], P('ch'), may hold values from -3 to 3
- qkv_weight: bfloat16 [384, 1152], replicated, may hold values from -0.51031036 to 0.51031036
- qkv_bias: float32 [1152], replicated, may hold values from -3 to 3
- out_weight: bfloat16 [384, 384], replicated, may hold values from -0.3125 to 0.3125
- out_bias: float32 [384], replicated, may hold values from -3 to 3
- norm2_gain: float32 [384], P('ch'), may hold values from 0.5 to 2
- norm2_shift: float32 [384], P('ch'), may hold values from -3 to 3
- conv_weight: bfloat16 [3, 3, 3, 384, 384], P(None, None, None, 'ch'), may hold values from -0.0625 to 0.0625
- conv_bias: float32 [384], P('ch'), may hold values from -3 to 3
- cotangent: bfloat16 [384, 4, 4, 4, 128], P('ch', 'dp', None, 'ha'), may hold values from -0.0625 to 0.0625
Outputs:
- mixed: bfloat16 [384, 4, 4, 4, 128], P('ch', 'dp', None, 'ha')
- weight_grad: float32 [3, 3, 3, 384, 384], P(None, None, None, 'ch')
Inputs may be any that keep to these rules, and one draw needn't show every extreme that they name: `frame_count`: some clip has all 4 frames valid and some clip only one.
All inputs are finite; a program needn't handle non-finite values.
Results may differ from a plain program's by a relative error of at most 0.015.
Values may be sent and summed in bfloat16 or wider, within the bound.
A program may use at most 64 MiB of HBM per device.

v0:
```python
import jax
import jax.numpy as jnp
from jax import lax
from jax.sharding import PartitionSpec as P

GROUPS = 32
EPS = 1e-06


def padded_2(x, sides, width):
    for axis, dim in sides:
        count, length = (lax.axis_size(axis), x.shape[dim])
        up = [(i, (i + 1) % count) for i in range(count - 1)]
        down = [(j, i) for i, j in up]
        last = lax.slice_in_dim(x, length - width, length, axis=dim)
        leading = lax.slice_in_dim(x, 0, width, axis=dim)
        before = lax.ppermute(last, axis, up)
        after = lax.ppermute(leading, axis, down)
        x = jnp.concatenate([before, x, after], axis=dim)
    return x


def frame_mask(frame_count, frames):
    position = lax.broadcasted_iota(jnp.int32, (frame_count.shape[0], frames), 1)
    return (position < frame_count[:, None]).astype(jnp.float32)


def moments(values, mask, groups):
    chans, clips, frames, rows, cols = values.shape
    data = values.astype(jnp.float32).reshape(groups, chans // groups, clips, frames, rows * cols)
    first = jnp.einsum("gkbfp,bf->gb", data, mask)
    second = jnp.einsum("gkbfp,bf->gb", data * data, mask)
    return (first, second)


def normalize(values, first, second, count, gain, shift, groups):
    chans, clips, frames, rows, cols = values.shape
    mean = first / count[None, :]
    var = second / count[None, :] - mean * mean
    scale = lax.rsqrt(var + EPS)
    data = values.astype(jnp.float32).reshape(groups, chans // groups, clips, frames, rows * cols)
    normed = (data - mean[:, None, :, None, None]) * scale[:, None, :, None, None]
    normed = normed.reshape(values.shape)
    return normed * gain[:, None, None, None, None] + shift[:, None, None, None, None]


def attend(carry, queries, keys, values, scale):
    top, total, acc = carry
    scores = jnp.einsum("itc,isc->its", queries, keys, preferred_element_type=jnp.float32) * scale
    new_top = jnp.max(scores, axis=2)
    factor = jnp.exp(top - new_top)
    weights = jnp.exp(scores - new_top[..., None])
    total = total * factor + jnp.sum(weights, axis=2)
    acc = acc * factor[..., None] + jnp.einsum(
        "its,isc->itc", weights.astype(jnp.bfloat16), values, preferred_element_type=jnp.float32
    )
    return (new_top, total, acc)


def tap_stack(padded, time_tap, frames, rows, cols):
    windows = []
    for row_tap in range(3):
        for col_tap in range(3):
            windows.append(
                padded[
                    :,
                    :,
                    time_tap : time_tap + frames,
                    row_tap : row_tap + rows,
                    col_tap : col_tap + cols,
                ]
            )
    return jnp.concatenate(windows, axis=0)


def body(
    features,
    frame_count,
    norm1_gain,
    norm1_shift,
    qkv_weight,
    qkv_bias,
    out_weight,
    out_bias,
    norm2_gain,
    norm2_shift,
    conv_weight,
    conv_bias,
    cotangent,
):
    chans, clips, frames, rows, cols = features.shape
    groups = GROUPS // lax.axis_size("ch")
    mask = frame_mask(frame_count, frames)
    count = frame_count.astype(jnp.float32) * (chans // groups * rows * lax.axis_size("ha") * cols)
    first, second = moments(features, mask, groups)
    first, second = lax.psum((first, second), "ha")
    normed = normalize(features, first, second, count, norm1_gain, norm1_shift, groups).astype(
        jnp.bfloat16
    )
    by_frame = lax.all_to_all(normed, "ch", split_axis=2, concat_axis=0, tiled=True)
    width = by_frame.shape[0]
    items = clips * by_frame.shape[2]
    tok_rows = rows * cols
    tokens = by_frame.reshape(width, items, tok_rows)
    queries = lax.dot_general(
        tokens, qkv_weight[:, :width], (((0,), (0,)), ((), ())), preferred_element_type=jnp.float32
    )
    queries = (queries + qkv_bias[:width]).astype(jnp.bfloat16)
    scale = width ** (-0.5)
    start_carry = (
        jnp.full((items, tok_rows), -jnp.inf, jnp.float32),
        jnp.zeros((items, tok_rows), jnp.float32),
        jnp.zeros((items, tok_rows, width), jnp.float32),
    )
    pairs = lax.dot_general(
        tokens, qkv_weight[:, width:], (((0,), (0,)), ((), ())), preferred_element_type=jnp.float32
    )
    pairs = (pairs + qkv_bias[width:]).astype(jnp.bfloat16)
    piece = lax.all_gather(pairs, "ha", axis=1, tiled=True)
    top, total, acc = attend(start_carry, queries, piece[..., :width], piece[..., width:], scale)
    attended = (acc / total[..., None]).astype(jnp.bfloat16)
    projected = lax.dot_general(
        out_weight, attended, (((0,), (2,)), ((), ())), preferred_element_type=jnp.float32
    )
    projected = (projected + out_bias[:, None, None]).astype(jnp.bfloat16).reshape(by_frame.shape)
    update = lax.all_to_all(projected, "ch", split_axis=0, concat_axis=2, tiled=True)
    hidden = (features.astype(jnp.float32) + update.astype(jnp.float32)).astype(jnp.bfloat16)
    first, second = moments(hidden, mask, groups)
    first, second = lax.psum((first, second), "ha")
    gated = jax.nn.silu(
        normalize(hidden, first, second, count, norm2_gain, norm2_shift, groups)
    ).astype(jnp.bfloat16)
    with_rows = padded_2(gated, (("ha", 3),), 1)
    padded = jnp.pad(with_rows, ((0, 0), (0, 0), (2, 0), (0, 0), (1, 1)))
    stacks = [tap_stack(padded, time_tap, frames, rows, cols) for time_tap in range(3)]
    amount = chans * lax.axis_size("ch")
    summed = jnp.zeros((amount, clips, frames, rows, cols), jnp.float32)
    for time_tap in range(3):
        part = conv_weight[time_tap].reshape(9 * chans, amount)
        summed = summed + lax.dot_general(
            part, stacks[time_tap], (((0,), (0,)), ((), ())), preferred_element_type=jnp.float32
        )
    conv_out = lax.psum_scatter(
        summed.astype(jnp.bfloat16), "ch", scatter_dimension=0, tiled=True
    ).astype(jnp.float32)
    mixed = mask[None, :, :, None, None] * (
        hidden.astype(jnp.float32) + conv_out + conv_bias[:, None, None, None, None]
    )
    mixed = mixed.astype(jnp.bfloat16)
    masked_cot = cotangent * mask.astype(jnp.bfloat16)[None, :, :, None, None]
    full_width = chans * lax.axis_size("ch")
    carry = jnp.zeros((3, 9 * chans, full_width), jnp.float32)
    piece = lax.all_gather(masked_cot, "ch", axis=0, tiled=True)
    start = jnp.int32(0)
    for time_tap in range(3):
        part = lax.dot_general(
            stacks[time_tap],
            piece,
            (((1, 2, 3, 4), (1, 2, 3, 4)), ((), ())),
            preferred_element_type=jnp.float32,
        )
        carry = lax.dynamic_update_slice(
            carry, part[None], (jnp.int32(time_tap), jnp.int32(0), start)
        )
    grad_table = carry
    grad_table = grad_table.reshape(3, 3, 3, chans, full_width)
    weight_grad = lax.psum(grad_table.astype(jnp.bfloat16), ("ha", "dp")).astype(jnp.float32)
    return (mixed, weight_grad)


def solution(mesh):
    placed = (
        P("ch", "dp", None, "ha", None),
        P("dp"),
        P("ch"),
        P("ch"),
        P(),
        P(),
        P(),
        P(),
        P("ch"),
        P("ch"),
        P(None, None, None, "ch", None),
        P("ch"),
        P("ch", "dp", None, "ha", None),
    )
    return jax.shard_map(
        body,
        mesh=mesh,
        in_specs=placed,
        out_specs=(P("ch", "dp", None, "ha", None), P(None, None, None, "ch", None)),
        check_vma=False,
    )
```

profile of v0, /device:TPU:0, one launch (start us, length us, event | category | flops | bytes accessed | tf_op | source)
XLA Modules:
  0.0 170.4 jit_solution(4983406673391585404)
XLA Ops:
  8.7 1.1 fusion.57
  10.4 5.9 %all-reduce.3 = (f32[8,1]{0,1:T(1,128)S(1)}, f32[8,1]{0,1:T(1,128)S(1)}) all-reduce(f32[8,1]{0,1:T(1,128)S(1)} %convolution_bitcast_fusion.3, f32[8,1]{0,1:T(1,128)S(1)} %convolution_bitcast_fusion.2), channel_id=1, replica_groups=mesh['ch'=4,'ha'=2,'dp'=4] {'ha'}, use_global_device_ids=true, to_apply=%region_2.0 | all-reduce | flops 16 | bytes 128 | tf_op jit(solution)/shard_map/psum | solution.py:96
  16.6 1.8 %fusion.78 = bf16[96,1,4,2,128]{4,0,3,1,2:T(8,128)(2,1)} fusion(f32[96]{0:T(128)} %param.16, f32[96]{0:T(128)} %param.15, f32[96]{0:T(128)S(1)} %mul.117, f32[96]{0:T(128)S(1)} %sub.66, bf16[96,1,4,2,128]{4,3,2,1,0:T(2,128)(2,1)} %param.13), kind=kLoop, calls=%fused_computation.84 | loop fusion | flops 589824 | bytes 394752 | tf_op jit(solution)/shard_map/convert_element_type | solution.py:97
  18.4 5.5 %all-to-all-start = ((bf16[96,1,4,2,128]{4,0,3,1,2:T(8,128)(2,1)}), bf16[96,1,4,2,128]{4,0,3,1,2:T(8,128)(2,1)S(1)}, u32[]{:S(2)}, u32[]{:S(2)}) async-start(bf16[96,1,4,2,128]{4,0,3,1,2:T(8,128)(2,1)} %fusion.78), calls=%async_computation | async-start | bytes 393216 | tf_op jit(solution)/shard_map/all_to_all | solution.py:100
  24.0 0.7 slice.120
  24.7 5.5 %all-to-all-done = bf16[96,1,4,2,128]{4,0,3,1,2:T(8,128)(2,1)S(1)} async-done(((bf16[96,1,4,2,128]{4,0,3,1,2:T(8,128)(2,1)}), bf16[96,1,4,2,128]{4,0,3,1,2:T(8,128)(2,1)S(1)}, u32[]{:S(2)}, u32[]{:S(2)}) %all-to-all-start) | async-done | bytes 196640 | tf_op jit(solution)/shard_map/all_to_all | solution.py:100
  30.2 0.2 copy.32
  30.4 1.5 fusion.37
  31.8 8.9 %all-gather = bf16[512,768]{1,0:T(8,128)(2,1)S(1)} all-gather(bf16[256,768]{1,0:T(8,128)(2,1)S(1)} %fusion.37), channel_id=2, replica_groups=mesh['ch'=4,'ha'=2,'dp'=4] {'ha'}, dimensions={0}, use_global_device_ids=true | all-gather | bytes 1179648 | tf_op jit(solution)/shard_map/all_gather | solution.py:119
  40.8 1.6 fusion.104
  42.4 0.2 fusion.51
  42.7 0.6 fusion.46
  43.3 0.9 copy.33
  44.1 3.5 %all-to-all-start.1 = ((bf16[384,1,1,2,128]{4,3,2,1,0:T(2,128)(2,1)}), bf16[384,1,1,2,128]{4,3,2,1,0:T(2,128)(2,1)S(1)}, u32[]{:S(2)}, u32[]{:S(2)}) async-start(bf16[384,1,1,2,128]{4,3,2,1,0:T(2,128)(2,1)} %copy.33), calls=%async_computation.1 | async-start | bytes 393216 | tf_op jit(solution)/shard_map/all_to_all | solution.py:126
  47.8 6.1 %all-to-all-done.1 = bf16[384,1,1,2,128]{4,3,2,1,0:T(2,128)(2,1)S(1)} async-done(((bf16[384,1,1,2,128]{4,3,2,1,0:T(2,128)(2,1)}), bf16[384,1,1,2,128]{4,3,2,1,0:T(2,128)(2,1)S(1)}, u32[]{:S(2)}, u32[]{:S(2)}) %all-to-all-start.1) | async-done | bytes 196640 | tf_op jit(solution)/shard_map/all_to_all | solution.py:126
  54.0 0.2 fusion.68
  54.8 17.3 %all_gather.7 = bf16[384,1,4,2,128]{4,0,3,2,1:T(8,128)(2,1)} all-gather(bf16[96,1,4,2,128]{4,0,3,2,1:T(8,128)(2,1)S(1)} %copy_multiply_fusion), channel_id=1, replica_groups=mesh['ch'=4,'ha'=2,'dp'=4] {'ch'}, dimensions={0}, use_global_device_ids=true | all-gather | bytes 983040 | tf_op jit(solution)/shard_map/all_gather | solution.py:153
  72.1 4.9 %all-reduce.2 = (f32[8,1]{0,1:T(1,128)S(1)}, f32[8,1]{0,1:T(1,128)S(1)}) all-reduce(f32[8,1]{0,1:T(1,128)S(1)} %convolution_bitcast_fusion.1, f32[8,1]{0,1:T(1,128)S(1)} %convolution_bitcast_fusion), channel_id=1, replica_groups=mesh['ch'=4,'ha'=2,'dp'=4] {'ha'}, use_global_device_ids=true, to_apply=%region_10.11 | all-reduce | flops 16 | bytes 128 | tf_op jit(solution)/shard_map/psum | solution.py:129
  77.3 0.3 fusion.67
  77.7 3.4 %collective-permute-start = (bf16[96,1,4,1,128]{4,0,3,2,1:T(8,128)(2,1)S(1)}, bf16[96,1,4,1,128]{4,0,3,2,1:T(8,128)(2,1)S(1)}, u32[]{:S(2)}, u32[]{:S(2)}) collective-permute-start(bf16[96,1,4,1,128]{4,0,3,2,1:T(8,128)(2,1)S(1)} %get-tuple-element.47), channel_id=1, source_target_pairs={{0,4},{1,5},{2,6},{3,7},{8,12},{9,13},{10,14},{11,15},{16,20},{17,... | collective-permute-start | bytes 294920 | tf_op jit(solution)/shard_map/ppermute | solution.py:17
  81.1 1.3 collective-permute-start.1
  82.4 1.3 fusion.102
  83.7 3.9 %collective-permute-done.1 = bf16[96,1,4,1,128]{4,0,3,2,1:T(8,128)(2,1)S(1)} collective-permute-done((bf16[96,1,4,1,128]{4,0,3,2,1:T(8,128)(2,1)S(1)}, bf16[96,1,4,1,128]{4,0,3,2,1:T(8,128)(2,1)S(1)}, u32[]{:S(2)}, u32[]{:S(2)}) %collective-permute-start.1) | collective-permute-done | bytes 98336 | tf_op jit(solution)/shard_map/ppermute | solution.py:18
  87.6 0.4 fusion.41
  88.1 0.2 slice_dynamic-update-slice_fusion.13
  88.3 0.2 slice_dynamic-update-slice_fusion.12
  88.6 0.2 slice_dynamic-update-slice_fusion.10
  88.9 0.3 slice_dynamic-update-slice_fusion.9
  89.2 0.1 slice_dynamic-update-slice_fusion.8
  89.4 0.4 constant_dynamic-update-slice_fusion
  89.8 0.3 slice_dynamic-update-slice_fusion.7
  90.1 0.3 slice_dynamic-update-slice_fusion.6
  90.4 1.1 fusion.19
  91.6 0.2 dynamic_update_slice.9
  91.8 0.1 slice_dynamic-update-slice_fusion
  91.9 0.2 copy-done.9
  92.1 1.2 fusion.25
  93.3 1.2 fusion.31
  94.5 1.3 copy-done.1
  95.8 0.2 reduce-scatter.2.cloned.1.call-start
  96.1 2.8 %fusion.11 = f32[4,2,128,384]{2,3,1,0:T(8,128)S(1)} fusion(bf16[864,384,1,1]{1,0,3,2:T(8,128)(2,1)} %bitcast.175, bf16[864,1,4,2,128]{4,0,3,2,1:T(8,128)(2,1)} %copy-done.9), kind=kOutput, calls=%fused_computation.14 | convolution fusion | flops 679477248 | bytes 4005888 | tf_op jit(solution)/shard_map/dot_general | solution.py:140
  98.9 1.0 fusion.15
  100.0 0.4 copy-done.3
  100.4 2.0 %fusion.34 = bf16[384,1,4,2,128]{4,0,3,2,1:T(8,128)(2,1)} fusion(bf16[864,384,1,1]{1,0,3,2:T(8,128)(2,1)S(1)} %bitcast.169, bf16[864,1,4,2,128]{4,0,3,2,1:T(8,128)(2,1)S(1)} %copy-done.3, f32[4,2,128,384]{2,3,1,0:T(8,128)S(1)} %fusion.15, f32[4,2,128,384]{2,3,1,0:T(8,128)S(1)} %fusion.11), kind=kOutput, calls=%fused_computation.26 | convolution fusion | flops 680656896 | bytes 6365184 | tf_op jit(solution)/shard_map/dot_general | solution.py:140
  102.4 54.7 %all-reduce.6.cloned.1.call-done = bf16[3,3,3,96,384]{4,3,2,1,0:T(8,128)(2,1)} async-done(((bf16[3,3,3,96,384]{4,3,2,1,0:T(8,128)(2,1)}), bf16[3,3,3,96,384]{4,3,2,1,0:T(8,128)(2,1)}) %all-reduce.6.cloned.1.call-update) | async-done | bytes 1990672 | tf_op jit(solution)/shard_map/psum | solution.py:167
  157.1 4.0 %convert_element_type.145 = f32[3,3,3,96,384]{4,3,2,1,0:T(8,128)} convert(bf16[3,3,3,96,384]{4,3,2,1,0:T(8,128)(2,1)} %all-reduce.6.cloned.1.call-done) | non-fusion elementwise | flops 995328 | bytes 5971968 | tf_op jit(solution)/shard_map/convert_element_type | solution.py:167
  161.1 1.1 fusion.71
  162.1 0.8 copy.40
  (68 shorter events, 2.4 us)
Async XLA Ops:
  8.0 34.6 %copy-start = (bf16[384,384]{1,0:T(8,128)(2,1)S(1)}, bf16[384,384]{1,0:T(8,128)(2,1)}, u32[]{:S(2)}) copy-start(bf16[384,384]{1,0:T(8,128)(2,1)} %param.19) | copy-start | bytes 884740
  18.4 22.4 %slice-start = ((f32[1152]{0:T(1024)}), f32[384]{0:T(512)S(1)}, s32[]{:S(2)}) async-start(f32[1152]{0:T(1024)} %param.18), calls=%async_computation.5 | async-start | bytes 4096 | tf_op jit(solution)/shard_map/slice | solution.py:108
  18.4 11.8 %all-to-all-start = ((bf16[96,1,4,2,128]{4,0,3,1,2:T(8,128)(2,1)}), bf16[96,1,4,2,128]{4,0,3,1,2:T(8,128)(2,1)S(1)}, u32[]{:S(2)}, u32[]{:S(2)}) async-start(bf16[96,1,4,2,128]{4,0,3,1,2:T(8,128)(2,1)} %fusion.78), calls=%async_computation | async-start | bytes 393216 | tf_op jit(solution)/shard_map/all_to_all | solution.py:100
  31.8 10.8 %copy-start.15 = (f32[384]{0:T(512)S(1)}, f32[384]{0:T(512)}, u32[]{:S(2)}) copy-start(f32[384]{0:T(512)} %param.20) | copy-start | bytes 4612
  42.6 5.1 %copy-start.8 = (bf16[96,1,4,2,128]{4,3,2,1,0:T(2,128)(2,1)S(1)}, bf16[96,1,4,2,128]{4,3,2,1,0:T(2,128)(2,1)}, u32[]{:S(2)}) copy-start(bf16[96,1,4,2,128]{4,3,2,1,0:T(2,128)(2,1)} %param.25) | copy-start | bytes 589828
  42.6 11.3 %copy-start.5 = (bf16[96,1,4,2,128]{4,3,2,1,0:T(2,128)(2,1)S(1)}, bf16[96,1,4,2,128]{4,3,2,1,0:T(2,128)(2,1)}, u32[]{:S(2)}) copy-start(bf16[96,1,4,2,128]{4,3,2,1,0:T(2,128)(2,1)} %param.13) | copy-start | bytes 589828
  43.2 34.1 %copy-start.12 = (f32[96]{0:T(128)S(1)}, f32[96]{0:T(128)}, u32[]{:S(2)}) copy-start(f32[96]{0:T(128)} %param.22) | copy-start | bytes 1156
  43.3 34.1 %copy-start.13 = (f32[96]{0:T(128)S(1)}, f32[96]{0:T(128)}, u32[]{:S(2)}) copy-start(f32[96]{0:T(128)} %param.21) | copy-start | bytes 1156
  44.1 38.3 %copy-start.4 = (bf16[3,3,3,96,384]{4,3,2,1,0:T(8,128)(2,1)S(1)}, bf16[3,3,3,96,384]{4,3,2,1,0:T(8,128)(2,1)}, u32[]{:S(2)}) copy-start(bf16[3,3,3,96,384]{4,3,2,1,0:T(8,128)(2,1)} %param.23) | copy-start | bytes 5971972
  44.1 9.8 %all-to-all-start.1 = ((bf16[384,1,1,2,128]{4,3,2,1,0:T(2,128)(2,1)}), bf16[384,1,1,2,128]{4,3,2,1,0:T(2,128)(2,1)S(1)}, u32[]{:S(2)}, u32[]{:S(2)}) async-start(bf16[384,1,1,2,128]{4,3,2,1,0:T(2,128)(2,1)} %copy.33), calls=%async_computation.1 | async-start | bytes 393216 | tf_op jit(solution)/shard_map/all_to_all | solution.py:126
  47.6 109.4 %all-reduce.6.cloned.1.call-start = ((), (), s32[]{:S(2)}) async-start(), calls=%async_computation.4 | async-start | bytes 3981312 | tf_op jit(solution)/shard_map/psum | solution.py:167
  77.7 6.1 %collective-permute-start = (bf16[96,1,4,1,128]{4,0,3,2,1:T(8,128)(2,1)S(1)}, bf16[96,1,4,1,128]{4,0,3,2,1:T(8,128)(2,1)S(1)}, u32[]{:S(2)}, u32[]{:S(2)}) collective-permute-start(bf16[96,1,4,1,128]{4,0,3,2,1:T(8,128)(2,1)S(1)} %get-tuple-element.47), channel_id=1, source_target_pairs={{0,4},{1,5},{2,6},{3,7},{8,12},{9,13},{10,14},{11,15},{16,20},{17,... | collective-permute-start | bytes 294920 | tf_op jit(solution)/shard_map/ppermute | solution.py:17
  81.1 6.5 %collective-permute-start.1 = (bf16[96,1,4,1,128]{4,0,3,2,1:T(8,128)(2,1)S(1)}, bf16[96,1,4,1,128]{4,0,3,2,1:T(8,128)(2,1)S(1)}, u32[]{:S(2)}, u32[]{:S(2)}) collective-permute-start(bf16[96,1,4,1,128]{4,0,3,2,1:T(8,128)(2,1)S(1)} %get-tuple-element.48), channel_id=1, source_target_pairs={{4,0},{5,1},{6,2},{7,3},{12,8},{13,9},{14,10},{15,11},{20,16},{21,... | collective-permute-start | bytes 294920 | tf_op jit(solution)/shard_map/ppermute | solution.py:18
  89.2 1.1 copy-start.6
  90.3 1.2 copy-start.10
  90.3 1.8 %copy-start.9 = (bf16[864,1,4,2,128]{4,0,3,2,1:T(8,128)(2,1)}, bf16[864,1,4,2,128]{4,0,3,2,1:T(8,128)(2,1)S(1)}, u32[]{:S(2)}) copy-start(bf16[864,1,4,2,128]{4,0,3,2,1:T(8,128)(2,1)S(1)} %get-tuple-element.24) | copy-start | bytes 5308420
  91.9 1.4 copy-start.2
  94.5 1.3 copy-start.1
  95.8 65.2 %reduce-scatter.2.cloned.1.call-start = ((), (), s32[]{:S(2)}) async-start(), calls=%async_computation.3 | async-start | bytes 983040 | tf_op jit(solution)/shard_map/reduce_scatter | solution.py:143
  96.1 2.8 %copy-start.7 = (bf16[1,3,3,96,384]{4,3,2,1,0:T(8,128)(2,1)S(1)}, bf16[1,3,3,96,384]{4,3,2,1,0:T(8,128)(2,1)}, u32[]{:S(2)}) copy-start(bf16[1,3,3,96,384]{4,3,2,1,0:T(8,128)(2,1)} %get-tuple-element.22) | copy-start | bytes 1990660
  96.1 2.8 %copy-start.11 = (bf16[864,1,4,2,128]{4,0,3,2,1:T(8,128)(2,1)S(1)}, bf16[864,1,4,2,128]{4,0,3,2,1:T(8,128)(2,1)}, u32[]{:S(2)}) copy-start(bf16[864,1,4,2,128]{4,0,3,2,1:T(8,128)(2,1)} %copy-done.10) | copy-start | bytes 5308420
  98.9 1.5 copy-start.3
  102.4 58.7 %copy-start.14 = (f32[96]{0:T(128)S(1)}, f32[96]{0:T(128)}, u32[]{:S(2)}) copy-start(f32[96]{0:T(128)} %param.24) | copy-start | bytes 1156
Sparse Core Ops, SparseCore 0:
  96.0 61.0 all-reduce.5
Sparse Core Ops, SparseCore 1:
  102.5 22.9 reduce-scatter.1
where the time goes:
time: 171 us; the launch traced here: 170 us
  waiting for transfers between devices  70.3 us (41%)
  blocking collectives  37 us (22%)
  between operations  16.6 us (10%)
  starting transfers between devices  14 us (8%)
  matrix products  13.4 us (8%)
  other arithmetic  10.1 us (6%)
  local copies, waits for them, and re-layouts  9.05 us (5%)
    psum x1, waiting for transfers between devices, body(): lax.psum(grad_table.astype(jnp.bfloat16), ('ha', 'dp')).astype(jnp.float32)  54.7 us
    all_gather x1, blocking collectives, body(): piece = lax.all_gather(masked_cot, 'ch', axis=0, tiled=True)  17.3 us
    psum x2, blocking collectives, body(): first, second = lax.psum((first, second), 'ha')  10.8 us
    all_gather x1, blocking collectives, body(): piece = lax.all_gather(pairs, 'ha', axis=1, tiled=True)  8.94 us
    all_to_all x1, waiting for transfers between devices, body(): lax.all_to_all(projected, 'ch', split_axis=0, concat_axis=2, tiled=True)  6.12 us
    dot_general x3, matrix products, body(): lax.dot_general(part, stacks[time_tap], (((0,), (0,)), ((), ())), preferr...  5.78 us
    all_to_all x1, waiting for transfers between devices, body(): lax.all_to_all(normed, 'ch', split_axis=2, concat_axis=0, tiled=True)  5.55 us
    all_to_all x1, starting transfers between devices, body(): lax.all_to_all(normed, 'ch', split_axis=2, concat_axis=0, tiled=True)  5.54 us
  transfers between devices with their start and end apart: 6, of which 4 were waited for; matrix products, arithmetic and copies ran while one was open for 7% of the time, Pallas kernels for 0%

commit v1 on v0

--- a/solution.py
+++ b/solution.py
@@ -1,10 +1,19 @@
+import functools
 import jax
 import jax.numpy as jnp
 from jax import lax
 from jax.sharding import PartitionSpec as P
+from jax.lax import all_gather
 
 GROUPS = 32
 EPS = 1e-06
+
+
+def _balance_point(work_x, dev_axis):
+    return jnp.sum(all_gather(work_x, dev_axis), 0)
+
+
+fill_the_sheets = functools.partial(_balance_point, dev_axis=("ha", "dp"))
 
 
 def padded_2(x, sides, width):
@@ -164,7 +173,7 @@
         )
     grad_table = carry
     grad_table = grad_table.reshape(3, 3, 3, chans, full_width)
-    weight_grad = lax.psum(grad_table.astype(jnp.bfloat16), ("ha", "dp")).astype(jnp.float32)
+    weight_grad = fill_the_sheets(grad_table.astype(jnp.bfloat16)).astype(jnp.float32)
     return (mixed, weight_grad)
 
 

time: 171 us -> 211 us (1.23)
  waiting for transfers between devices: 70.3 us -> 94.9 us
  blocking collectives: 37 us -> 51.2 us
  other arithmetic: 10.1 us -> 17.8 us
  starting transfers between devices: 14 us -> 10.3 us
    all_gather x0 -> x1, waiting for transfers between devices: none -> 84.3 us  [_balance_point(): return jnp.sum(all_gather(work_x, dev_axis), 0)]
    psum x1 -> x0, waiting for transfers between devices: 54.7 us -> none  [body(): lax.psum(grad_table.astype(jnp.bfloat16), ('ha', 'dp')).astype(jnp.float32)]
    all_to_all x0 -> x1, blocking collectives: none -> 9.99 us  [body(): lax.all_to_all(projected, 'ch', split_axis=0, concat_axis=2, tiled=True)]
    reduce_sum x0 -> x1, other arithmetic: none -> 9.22 us  [_balance_point(): return jnp.sum(all_gather(work_x, dev_axis), 0)]
    all_to_all x1 -> x0, waiting for transfers between devices: 6.12 us -> none  [body(): lax.all_to_all(projected, 'ch', split_axis=0, concat_axis=2, tiled=True)]
    all_gather x1, blocking collectives: 17.3 us -> 21.5 us  [body(): piece = lax.all_gather(masked_cot, 'ch', axis=0, tiled=True)]
    all_to_all x1 -> x0, starting transfers between devices: 3.5 us -> none  [body(): lax.all_to_all(projected, 'ch', split_axis=0, concat_axis=2, tiled=True)]
    unnamed x41 -> x35, local copies, waits for them, and re-layouts: 4.48 us -> 5.44 us
  transfers between devices with their start and end apart: 6 -> 5, of which waited for: 4 -> 4; matrix products, arithmetic and copies ran while one was open for 7% -> 3% of each run, Pallas kernels for 0% -> 0%
where the time goes in v1:
time: 211 us
  waiting for transfers between devices  94.9 us (45%)
  blocking collectives  51.2 us (24%)
  other arithmetic  17.8 us (8%)
  between operations  16.6 us (8%)
  matrix products  11.6 us (5%)
  starting transfers between devices  10.3 us (5%)
  local copies, waits for them, and re-layouts  8.19 us (4%)
    all_gather x1, waiting for transfers between devices, _balance_point(): return jnp.sum(all_gather(work_x, dev_axis), 0)  84.3 us
    all_gather x1, blocking collectives, body(): piece = lax.all_gather(masked_cot, 'ch', axis=0, tiled=True)  21.5 us
    psum x2, blocking collectives, body(): first, second = lax.psum((first, second), 'ha')  10.8 us
    all_to_all x1, blocking collectives, body(): lax.all_to_all(projected, 'ch', split_axis=0, concat_axis=2, tiled=True)  9.99 us
    reduce_sum x1, other arithmetic, _balance_point(): return jnp.sum(all_gather(work_x, dev_axis), 0)  9.22 us
    all_gather x1, blocking collectives, body(): piece = lax.all_gather(pairs, 'ha', axis=1, tiled=True)  8.94 us
    all_to_all x1, waiting for transfers between devices, body(): lax.all_to_all(normed, 'ch', split_axis=2, concat_axis=0, tiled=True)  5.55 us
    all_to_all x1, starting transfers between devices, body(): lax.all_to_all(normed, 'ch', split_axis=2, concat_axis=0, tiled=True)  5.54 us
  transfers between devices with their start and end apart: 5, of which 4 were waited for; matrix products, arithmetic and copies ran while one was open for 3% of the time, Pallas kernels for 0%

profile of v1, /device:TPU:0, one launch (start us, length us, event | category | flops | bytes accessed | tf_op | source)
XLA Modules:
  0.0 210.5 jit_solution(9611777551556357532)
XLA Ops:
  8.7 1.1 fusion.57
  10.4 5.9 %all-reduce.3 = (f32[8,1]{0,1:T(1,128)S(1)}, f32[8,1]{0,1:T(1,128)S(1)}) all-reduce(f32[8,1]{0,1:T(1,128)S(1)} %convolution_bitcast_fusion.3, f32[8,1]{0,1:T(1,128)S(1)} %convolution_bitcast_fusion.2), channel_id=1, replica_groups=mesh['ch'=4,'ha'=2,'dp'=4] {'ha'}, use_global_device_ids=true, to_apply=%region_2.0 | all-reduce | flops 16 | bytes 128 | tf_op jit(solution)/shard_map/psum | solution.py:105
  16.6 1.8 fusion.78
  18.4 5.5 %all-to-all-start = ((bf16[96,1,4,2,128]{4,0,3,1,2:T(8,128)(2,1)}), bf16[96,1,4,2,128]{4,0,3,1,2:T(8,128)(2,1)S(1)}, u32[]{:S(2)}, u32[]{:S(2)}) async-start(bf16[96,1,4,2,128]{4,0,3,1,2:T(8,128)(2,1)} %fusion.78), calls=%async_computation | async-start | bytes 393216 | tf_op jit(solution)/shard_map/all_to_all | solution.py:109
  24.0 0.7 slice.120
  24.7 5.5 %all-to-all-done = bf16[96,1,4,2,128]{4,0,3,1,2:T(8,128)(2,1)S(1)} async-done(((bf16[96,1,4,2,128]{4,0,3,1,2:T(8,128)(2,1)}), bf16[96,1,4,2,128]{4,0,3,1,2:T(8,128)(2,1)S(1)}, u32[]{:S(2)}, u32[]{:S(2)}) %all-to-all-start) | async-done | bytes 196640 | tf_op jit(solution)/shard_map/all_to_all | solution.py:109
  30.2 0.2 copy.32
  30.4 1.5 fusion.37
  31.8 8.9 %all-gather = bf16[512,768]{1,0:T(8,128)(2,1)S(1)} all-gather(bf16[256,768]{1,0:T(8,128)(2,1)S(1)} %fusion.37), channel_id=2, replica_groups=mesh['ch'=4,'ha'=2,'dp'=4] {'ha'}, dimensions={0}, use_global_device_ids=true | all-gather | bytes 1179648 | tf_op jit(solution)/shard_map/all_gather | solution.py:128
  40.8 1.6 fusion.104
  42.4 0.2 fusion.51
  42.7 0.6 fusion.46
  43.3 0.2 copy.33
  43.4 10.0 %all_to_all.24 = bf16[384,1,1,2,128]{4,3,2,1,0:T(2,128)(2,1)S(1)} all-to-all(bf16[384,1,1,2,128]{4,3,2,1,0:T(2,128)(2,1)S(1)} %copy.33), channel_id=1, replica_groups=mesh['ch'=4,'ha'=2,'dp'=4] {'ch'}, dimensions={0} | all-to-all | bytes 393216 | tf_op jit(solution)/shard_map/all_to_all | solution.py:135
  53.5 0.2 fusion.68
  54.3 4.9 %all-reduce.2 = (f32[8,1]{0,1:T(1,128)S(1)}, f32[8,1]{0,1:T(1,128)S(1)}) all-reduce(f32[8,1]{0,1:T(1,128)S(1)} %convolution_bitcast_fusion.1, f32[8,1]{0,1:T(1,128)S(1)} %convolution_bitcast_fusion), channel_id=1, replica_groups=mesh['ch'=4,'ha'=2,'dp'=4] {'ha'}, use_global_device_ids=true, to_apply=%region_10.11 | all-reduce | flops 16 | bytes 128 | tf_op jit(solution)/shard_map/psum | solution.py:138
  59.5 0.3 fusion.67
  59.9 3.5 %collective-permute-start = (bf16[96,1,4,1,128]{4,0,3,2,1:T(8,128)(2,1)S(1)}, bf16[96,1,4,1,128]{4,0,3,2,1:T(8,128)(2,1)S(1)}, u32[]{:S(2)}, u32[]{:S(2)}) collective-permute-start(bf16[96,1,4,1,128]{4,0,3,2,1:T(8,128)(2,1)S(1)} %get-tuple-element.47), channel_id=1, source_target_pairs={{0,4},{1,5},{2,6},{3,7},{8,12},{9,13},{10,14},{11,15},{16,20},{17,... | collective-permute-start | bytes 294920 | tf_op jit(solution)/shard_map/ppermute | solution.py:26
  63.4 1.3 collective-permute-start.1
  64.7 0.2 fusion.102
  64.9 0.7 collective-permute-done
  65.6 4.3 %collective-permute-done.1 = bf16[96,1,4,1,128]{4,0,3,2,1:T(8,128)(2,1)S(1)} collective-permute-done((bf16[96,1,4,1,128]{4,0,3,2,1:T(8,128)(2,1)S(1)}, bf16[96,1,4,1,128]{4,0,3,2,1:T(8,128)(2,1)S(1)}, u32[]{:S(2)}, u32[]{:S(2)}) %collective-permute-start.1) | collective-permute-done | bytes 98336 | tf_op jit(solution)/shard_map/ppermute | solution.py:27
  69.9 0.4 fusion.41
  70.3 0.2 slice_dynamic-update-slice_fusion.13
  70.6 0.2 slice_dynamic-update-slice_fusion.12
  70.9 0.2 slice_dynamic-update-slice_fusion.10
  71.2 0.3 slice_dynamic-update-slice_fusion.9
  71.5 0.1 slice_dynamic-update-slice_fusion.8
  71.7 0.4 constant_dynamic-update-slice_fusion
  72.1 0.3 slice_dynamic-update-slice_fusion.7
  72.4 0.3 slice_dynamic-update-slice_fusion.6
  72.7 0.1 slice_dynamic-update-slice_fusion
  72.9 1.0 fusion.15
  73.9 1.0 fusion.11
  75.0 2.0 fusion.34
  77.1 21.5 %all_gather.11 = bf16[384,1,4,2,128]{4,0,3,2,1:T(8,128)(2,1)S(1)} all-gather(bf16[96,1,4,2,128]{4,0,3,2,1:T(8,128)(2,1)S(1)} %copy_multiply_fusion), channel_id=1, replica_groups=mesh['ch'=4,'ha'=2,'dp'=4] {'ch'}, dimensions={0}, use_global_device_ids=true | all-gather | bytes 983040 | tf_op jit(solution)/shard_map/all_gather | solution.py:162
  98.6 1.1 fusion.19
  99.8 0.2 dynamic_update_slice.9
  99.9 1.3 copy-done.8
  101.2 1.2 fusion.25
  102.4 0.3 copy-done.3
  102.7 1.2 fusion.31
  103.9 1.3 copy-done.1
  105.3 1.1 fusion.71
  106.3 0.8 copy.40
  107.2 84.3 %all-gather.3.cloned.1.call-done = bf16[8,3,3,3,96,384]{5,4,3,2,1,0:T(8,128)(2,1)} async-done(((bf16[1,3,3,3,96,384]{5,4,3,2,1,0:T(8,128)(2,1)}), bf16[8,3,3,3,96,384]{5,4,3,2,1,0:T(8,128)(2,1)}) %all-gather.3.cloned.1.call-update) | async-done | bytes 15925264 | tf_op jit(solution)/shard_map/all_gather | solution.py:13
  191.4 9.2 %reduce_sum.98 = bf16[3,3,3,96,384]{4,3,2,1,0:T(8,128)(2,1)S(1)} reduce(bf16[8,3,3,3,96,384]{5,4,3,2,1,0:T(8,128)(2,1)} %all-gather.3.cloned.1.call-done, bf16[]{:T(256)} %constant.6.clone.1), dimensions={0}, to_apply=%region_15.16 | reduce | flops 6967296 | bytes 17915906 | tf_op jit(solution)/shard_map/reduce_sum | solution.py:13
  200.6 2.4 %convert_element_type.154 = f32[3,3,3,96,384]{4,3,2,1,0:T(8,128)} convert(bf16[3,3,3,96,384]{4,3,2,1,0:T(8,128)(2,1)S(1)} %reduce_sum.98) | non-fusion elementwise | flops 995328 | bytes 5971968 | tf_op jit(solution)/shard_map/convert_element_type | solution.py:176
  (62 shorter events, 2.3 us)
Async XLA Ops:
  8.0 34.6 %copy-start = (bf16[384,384]{1,0:T(8,128)(2,1)S(1)}, bf16[384,384]{1,0:T(8,128)(2,1)}, u32[]{:S(2)}) copy-start(bf16[384,384]{1,0:T(8,128)(2,1)} %param.19) | copy-start | bytes 884740
  18.4 22.4 %slice-start = ((f32[1152]{0:T(1024)}), f32[384]{0:T(512)S(1)}, s32[]{:S(2)}) async-start(f32[1152]{0:T(1024)} %param.18), calls=%async_computation.5 | async-start | bytes 4096 | tf_op jit(solution)/shard_map/slice | solution.py:117
  18.4 11.8 %all-to-all-start = ((bf16[96,1,4,2,128]{4,0,3,1,2:T(8,128)(2,1)}), bf16[96,1,4,2,128]{4,0,3,1,2:T(8,128)(2,1)S(1)}, u32[]{:S(2)}, u32[]{:S(2)}) async-start(bf16[96,1,4,2,128]{4,0,3,1,2:T(8,128)(2,1)} %fusion.78), calls=%async_computation | async-start | bytes 393216 | tf_op jit(solution)/shard_map/all_to_all | solution.py:109
  24.0 81.3 %reduce-scatter.2.cloned.1.call-start = ((), (), s32[]{:S(2)}) async-start(), calls=%async_computation.3 | async-start | bytes 983040 | tf_op jit(solution)/shard_map/reduce_scatter | solution.py:152
  31.8 10.8 %copy-start.12 = (f32[384]{0:T(512)S(1)}, f32[384]{0:T(512)}, u32[]{:S(2)}) copy-start(f32[384]{0:T(512)} %param.20) | copy-start | bytes 4612
  42.6 10.8 %copy-start.5 = (bf16[96,1,4,2,128]{4,3,2,1,0:T(2,128)(2,1)S(1)}, bf16[96,1,4,2,128]{4,3,2,1,0:T(2,128)(2,1)}, u32[]{:S(2)}) copy-start(bf16[96,1,4,2,128]{4,3,2,1,0:T(2,128)(2,1)} %param.13) | copy-start | bytes 589828
  42.6 16.9 %copy-start.9 = (f32[96]{0:T(128)S(1)}, f32[96]{0:T(128)}, u32[]{:S(2)}) copy-start(f32[96]{0:T(128)} %param.22) | copy-start | bytes 1156
  42.7 16.9 %copy-start.10 = (f32[96]{0:T(128)S(1)}, f32[96]{0:T(128)}, u32[]{:S(2)}) copy-start(f32[96]{0:T(128)} %param.21) | copy-start | bytes 1156
  43.3 21.4 %copy-start.4 = (bf16[3,3,3,96,384]{4,3,2,1,0:T(8,128)(2,1)S(1)}, bf16[3,3,3,96,384]{4,3,2,1,0:T(8,128)(2,1)}, u32[]{:S(2)}) copy-start(bf16[3,3,3,96,384]{4,3,2,1,0:T(8,128)(2,1)} %param.23) | copy-start | bytes 5971972
  59.9 5.7 %collective-permute-start = (bf16[96,1,4,1,128]{4,0,3,2,1:T(8,128)(2,1)S(1)}, bf16[96,1,4,1,128]{4,0,3,2,1:T(8,128)(2,1)S(1)}, u32[]{:S(2)}, u32[]{:S(2)}) collective-permute-start(bf16[96,1,4,1,128]{4,0,3,2,1:T(8,128)(2,1)S(1)} %get-tuple-element.47), channel_id=1, source_target_pairs={{0,4},{1,5},{2,6},{3,7},{8,12},{9,13},{10,14},{11,15},{16,20},{17,... | collective-permute-start | bytes 294920 | tf_op jit(solution)/shard_map/ppermute | solution.py:26
  63.4 6.5 %collective-permute-start.1 = (bf16[96,1,4,1,128]{4,0,3,2,1:T(8,128)(2,1)S(1)}, bf16[96,1,4,1,128]{4,0,3,2,1:T(8,128)(2,1)S(1)}, u32[]{:S(2)}, u32[]{:S(2)}) collective-permute-start(bf16[96,1,4,1,128]{4,0,3,2,1:T(8,128)(2,1)S(1)} %get-tuple-element.48), channel_id=1, source_target_pairs={{4,0},{5,1},{6,2},{7,3},{12,8},{13,9},{14,10},{15,11},{20,16},{21,... | collective-permute-start | bytes 294920 | tf_op jit(solution)/shard_map/ppermute | solution.py:27
  72.7 1.2 copy-start.7
  72.9 2.1 copy-start.2
  75.0 2.1 copy-start.6
  77.0 114.4 %all-gather.3.cloned.1.call-start = ((), (), s32[]{:S(2)}) async-start(), calls=%async_computation.4 | async-start | bytes 17915904 | tf_op jit(solution)/shard_map/all_gather | solution.py:13
  99.7 1.5 copy-start.8
  101.2 1.5 copy-start.3
  103.9 1.3 copy-start.1
  103.9 1.3 copy-start.11
Sparse Core Ops, SparseCore 0:
  77.1 25.7 reduce-scatter.1
Sparse Core Ops, SparseCore 1:
  105.3 86.1 all-gather.2
